TPU v7x, 512 devices: a whole 4x8x8 slice. The times are simulated.
512 devices in a mesh: expert: 8 (over y), tensor: 64 (over z, x, core).
Axes of the slice: x: 4, y: 8, z: 8, core: 2. Of those that a mesh axis runs over, the one named last changes fastest.
Arguments:
- expert_hidden: bfloat16 [8, 768, 8192], P('expert', 'tensor'), may hold values from -6 to 6
- probe_tangent: bfloat16 [8, 6144, 8192], P('expert', 'tensor'), may hold values from -0.0625 to 0.0625
- routed_experts: int32 [1536, 2], P('expert'), may hold values from 0 to 7, all different within a row; in each aligned block of 192 rows (0 to 191, 192 to 383, ...) at most 96 rows name the same one
- gate_weights: float32 [1536, 2], P('expert'), may hold values from 0.1 to 1
Outputs:
- ggn_product: bfloat16 [8, 6144, 8192], P('expert', 'tensor')
- token_quadratic: float32 [1536], P('expert')
Inputs may be any that keep to these rules, and one draw needn't show every extreme that they name: `routed_experts`: each row names two different experts. Among the 192 rows of one source, no expert is named by more than 96 rows, a bound that some block reaches.
All inputs are finite; a program needn't handle non-finite values.
Results may differ from a plain program's by a relative error of at most 0.0057.
Values may be sent and summed in bfloat16 or wider, within the bound.
No kernel may reach another device: no remote copies, remote signals or barrier semaphores. Data moves between devices by JAX's collectives and lax.ppermute only.
A program may use at most 128 MiB of HBM per device.

v0:
```python
import jax
import jax.numpy as jnp
from jax import lax
from jax.sharding import PartitionSpec as P


def local(expert_hidden, probe_tangent, routed_experts, gate_weights):
    expert_count = lax.axis_size("expert")
    tensor_count = lax.axis_size("tensor")
    hidden_local = expert_hidden[0]
    probe_local = probe_tangent[0]
    col_count = probe_local.shape[0]
    tok_count = routed_experts.shape[0]
    capacity = hidden_local.shape[0] * tensor_count // expert_count
    ids_flat = routed_experts.reshape(-1)
    gate_flat = gate_weights.reshape(-1)
    one_hot = (ids_flat[:, None] == jnp.arange(expert_count, dtype=jnp.int32)[None, :]).astype(
        jnp.int32
    )
    earlier = jnp.cumsum(one_hot, axis=0) - one_hot
    slot_rank = jnp.sum(one_hot * earlier, axis=1)
    buffer_row = ids_flat * capacity + slot_rank
    hidden_all = lax.all_gather(hidden_local, "tensor", axis=0, tiled=True)
    expert_tangent = lax.dot_general(
        hidden_all, probe_local, (((1,), (1,)), ((), ())), preferred_element_type=jnp.float32
    ).astype(jnp.bfloat16)
    outgoing = expert_tangent.reshape(expert_count, capacity, col_count)
    received = lax.all_to_all(outgoing, "expert", split_axis=0, concat_axis=0, tiled=True)
    block_cols = received.shape[2]
    flat_rows = received.reshape(expert_count * capacity, block_cols)
    picked = flat_rows[buffer_row].astype(jnp.float32) * gate_flat[:, None]
    token_tangent = jnp.sum(picked.reshape(tok_count, 2, block_cols), axis=1)
    weighted = (token_tangent[:, None, :] * gate_weights[:, :, None]).reshape(
        tok_count * 2, block_cols
    )
    weighted = weighted.astype(jnp.bfloat16)
    buffer = (
        jnp.zeros((expert_count * capacity, block_cols), jnp.bfloat16).at[buffer_row].set(weighted)
    )
    buffer, token_tangent = (buffer, token_tangent)
    returning = lax.all_to_all(
        buffer.reshape(expert_count, capacity, col_count),
        "expert",
        split_axis=0,
        concat_axis=0,
        tiled=True,
    )
    returning_flat = returning.reshape(expert_count * capacity, col_count)
    gradient = lax.dot_general(
        returning_flat, hidden_all, (((0,), (0,)), ((), ())), preferred_element_type=jnp.float32
    ).astype(jnp.bfloat16)
    partial_squares = jnp.sum(token_tangent * token_tangent, axis=1)
    total_squares = lax.psum(partial_squares, "tensor")
    token_quadratic = total_squares / (col_count * tensor_count)
    return (gradient[None], token_quadratic)


def solution(mesh):
    placed = (
        P("expert", "tensor", None),
        P("expert", "tensor", None),
        P("expert", None),
        P("expert", None),
    )
    return jax.shard_map(
        local,
        mesh=mesh,
        in_specs=placed,
        out_specs=(P("expert", "tensor", None), P("expert")),
        check_vma=False,
    )
```

profile of v0, /device:TPU:1, one launch (start us, length us, event | category | flops | bytes accessed | tf_op | source)
XLA Modules:
  0.0 347.5 jit_solution(15207525154912715444)
XLA Ops:
  7.2 0.0 copy-start
  7.2 0.0 copy-start.1
  7.2 0.0 all-gather.3.cloned.1.call-start
  7.2 2.1 copy.33
  9.4 0.0 all-gather.3.cloned.1.call-update
  9.4 0.8 copy.31
  10.2 0.1 eq.29
  10.3 0.1 eq.25
  10.5 0.9 reduce-window.6
  11.4 0.2 slice_reduce_fusion
  11.6 0.7 broadcast_multiply_fusion
  12.3 132.1 %all-gather.3.cloned.1.call-done = bf16[1,768,8192]{2,0,1:T(2,128)(2,1)} async-done(((bf16[1,12,8192]{2,0,1:T(2,128)(2,1)}), bf16[1,768,8192]{2,0,1:T(2,128)(2,1)}) %all-gather.3.cloned.1.call-update) | async-done | bytes 12582928 | tf_op jit(solution)/shard_map/all_gather | solution.py:23
  144.4 0.0 copy-done
  144.4 22.4 %fusion.13 = bf16[768,96]{0,1:T(8,128)(2,1)S(1)} fusion(bf16[1,96,8192]{2,1,0:T(8,128)(2,1)S(1)} %copy-done, bf16[1,768,8192]{2,0,1:T(2,128)(2,1)} %all-gather.3.cloned.1.call-done), kind=kOutput, calls=%fused_computation.11 | convolution fusion | flops 1208033280 | bytes 14303232 | tf_op jit(solution)/shard_map/dot_general | solution.py:24
  166.8 0.2 reshape.79
  167.0 0.7 copy.34
  167.7 6.5 %all-to-all-start = ((bf16[8,96,96]{1,2,0:T(8,128)(2,1)}), bf16[8,96,96]{1,2,0:T(8,128)(2,1)S(1)}, u32[]{:S(2)}, u32[]{:S(2)}) async-start(bf16[8,96,96]{1,2,0:T(8,128)(2,1)} %copy.34), calls=%async_computation | async-start | bytes 393216 | tf_op jit(solution)/shard_map/all_to_all | solution.py:28
  174.2 0.1 fusion.23
  174.3 0.1 copy.30
  174.4 0.1 mul.51
  174.5 0.0 copy-done.1
  174.6 0.1 copy.36
  174.7 0.1 mul.57
  174.9 8.9 %all-to-all-done = bf16[8,96,96]{1,2,0:T(8,128)(2,1)S(1)} async-done(((bf16[8,96,96]{1,2,0:T(8,128)(2,1)}), bf16[8,96,96]{1,2,0:T(8,128)(2,1)S(1)}, u32[]{:S(2)}, u32[]{:S(2)}) %all-to-all-start) | async-done | bytes 147488 | tf_op jit(solution)/shard_map/all_to_all | solution.py:28
  183.8 0.1 copy.35
  183.9 1.4 gather_fusion
  185.4 0.3 fusion.18
  185.7 0.1 mul.55
  185.8 2.2 scatter_custom_fusion
  188.0 3.4 all-to-all-start.1
  191.4 0.1 multiply_reduce_fusion
  191.5 125.3 %psum.7 = f32[192]{0:T(256)S(1)} all-reduce(f32[192]{0:T(256)S(1)} %multiply_reduce_fusion), channel_id=1, replica_groups=mesh['expert'=8,'tensor'=64] {'tensor'}, use_global_device_ids=true, to_apply=%region_6.7 | all-reduce | flops 192 | bytes 1536 | tf_op jit(solution)/shard_map/psum | solution.py:53
  316.8 0.6 broadcast_multiply_fusion.1
  317.3 0.0 all-to-all-done.1
  317.3 23.3 %fusion.7 = bf16[1,96,8192]{2,1,0:T(8,128)(2,1)} fusion(bf16[768,96]{1,0:T(8,128)(2,1)S(1)} %bitcast.38, bf16[1,768,8192]{2,0,1:T(2,128)(2,1)} %all-gather.3.cloned.1.call-done), kind=kOutput, calls=%fused_computation.7 | convolution fusion | flops 1208745984 | bytes 14303232 | tf_op jit(solution)/shard_map/dot_general | solution.py:49
  (4 shorter events, 0.1 us)
Async XLA Ops:
  7.2 137.2 %copy-start = (bf16[1,96,8192]{2,1,0:T(8,128)(2,1)S(1)}, bf16[1,96,8192]{2,1,0:T(8,128)(2,1)}, u32[]{:S(2)}) copy-start(bf16[1,96,8192]{2,1,0:T(8,128)(2,1)} %param.5) | copy-start | bytes 4718596
  7.2 167.4 %copy-start.1 = (f32[192,2]{0,1:T(2,128)S(1)}, f32[192,2]{0,1:T(2,128)}, u32[]{:S(2)}) copy-start(f32[192,2]{0,1:T(2,128)} %param.7) | copy-start | bytes 4612
  7.2 137.2 %all-gather.3.cloned.1.call-start = ((), (), s32[]{:S(2)}) async-start(), calls=%async_computation.2 | async-start | bytes 25559040 | tf_op jit(solution)/shard_map/all_gather | solution.py:23
  167.7 16.0 %all-to-all-start = ((bf16[8,96,96]{1,2,0:T(8,128)(2,1)}), bf16[8,96,96]{1,2,0:T(8,128)(2,1)S(1)}, u32[]{:S(2)}, u32[]{:S(2)}) async-start(bf16[8,96,96]{1,2,0:T(8,128)(2,1)} %copy.34), calls=%async_computation | async-start | bytes 393216 | tf_op jit(solution)/shard_map/all_to_all | solution.py:28
  188.0 129.3 %all-to-all-start.1 = ((bf16[8,96,96]{2,1,0:T(8,128)(2,1)}), bf16[8,96,96]{2,1,0:T(8,128)(2,1)S(1)}, u32[]{:S(2)}, u32[]{:S(2)}) async-start(bf16[8,96,96]{2,1,0:T(8,128)(2,1)} %bitcast.6), calls=%async_computation.1 | async-start | bytes 393216 | tf_op jit(solution)/shard_map/all_to_all | solution.py:41
Sparse Core Ops, SparseCore 0:
  11.9 132.4 all-gather.2
where the time goes:
time: 348 us
  waiting for transfers between devices  141 us (41%)
  blocking collectives  125 us (36%)
  matrix products  45.7 us (13%)
  between operations  14.2 us (4%)
  starting transfers between devices  9.89 us (3%)
  local copies, waits for them, and re-layouts  6.58 us (2%)
  other arithmetic  4.95 us (1%)
    all_gather x1, waiting for transfers between devices, local(): hidden_all = lax.all_gather(hidden_local, 'tensor', axis=0, tiled=True)  132 us
    psum x1, blocking collectives, local(): total_squares = lax.psum(partial_squares, 'tensor')  125 us
    dot_general x1, matrix products, local(): lax.dot_general(returning_flat, hidden_all, (((0,), (0,)), ((), ())), pre...  23.3 us
    dot_general x1, matrix products, local(): lax.dot_general(hidden_all, probe_local, (((1,), (1,)), ((), ())), prefer...  22.4 us
    all_to_all x1, waiting for transfers between devices, local(): lax.all_to_all(outgoing, 'expert', split_axis=0, concat_axis=0, tiled=True)  8.9 us
  transfers between devices with their start and end apart: 3, of which 2 were waited for; matrix products, arithmetic and copies ran while one was open for 1% of the time, Pallas kernels for 0%

commit v1 on v0

--- a/solution.py
+++ b/solution.py
@@ -1,7 +1,20 @@
+import functools
 import jax
 import jax.numpy as jnp
 from jax import lax
 from jax.sharding import PartitionSpec as P
+
+
+def use_numbers(tile_in, chip_axis):
+    return jnp.concatenate(
+        lax.all_to_all(
+            jnp.stack([tile_in for _ in range(lax.axis_size(chip_axis))]), chip_axis, 0, 0
+        ),
+        axis=0,
+    )
+
+
+post_ways = functools.partial(use_numbers, chip_axis="tensor")
 
 
 def local(expert_hidden, probe_tangent, routed_experts, gate_weights):
@@ -20,7 +33,7 @@
     earlier = jnp.cumsum(one_hot, axis=0) - one_hot
     slot_rank = jnp.sum(one_hot * earlier, axis=1)
     buffer_row = ids_flat * capacity + slot_rank
-    hidden_all = lax.all_gather(hidden_local, "tensor", axis=0, tiled=True)
+    hidden_all = post_ways(hidden_local)
     expert_tangent = lax.dot_general(
         hidden_all, probe_local, (((1,), (1,)), ((), ())), preferred_element_type=jnp.float32
     ).astype(jnp.bfloat16)

time: 348 us -> 572 us (1.64)
  waiting for transfers between devices: 141 us -> 371 us
  matrix products: 45.7 us -> 16.5 us
  local copies, waits for them, and re-layouts: 6.58 us -> 27.4 us
  starting transfers between devices: 9.89 us -> 25.4 us
  between operations: 14.2 us -> 0.78 us
    all_to_all x0 -> x1, waiting for transfers between devices: none -> 361 us  [use_numbers(): lax.all_to_all(jnp.stack([tile_in for _ in range(lax.axis_size(chip_axis)...]
    all_gather x1 -> x0, waiting for transfers between devices: 132 us -> none  [local(): hidden_all = lax.all_gather(hidden_local, 'tensor', axis=0, tiled=True)]
    reshape x0 -> x1, local copies, waits for them, and re-layouts: none -> 16.8 us  [use_numbers(): jnp.concatenate(lax.all_to_all(jnp.stack([tile_in for _ in range(lax.axis...]
    dot_general x1, matrix products: 23.3 us -> 7.9 us  [local(): lax.dot_general(returning_flat, hidden_all, (((0,), (0,)), ((), ())), pre...]
    all_to_all x0 -> x1, starting transfers between devices: none -> 15.1 us  [use_numbers(): lax.all_to_all(jnp.stack([tile_in for _ in range(lax.axis_size(chip_axis)...]
    dot_general x1, matrix products: 22.4 us -> 8.58 us  [local(): lax.dot_general(hidden_all, probe_local, (((1,), (1,)), ((), ())), prefer...]
    another operation x0 -> x1, local copies, waits for them, and re-layouts: none -> 6.81 us  [use_numbers(): jnp.stack([tile_in for _ in range(lax.axis_size(chip_axis))])]
  transfers between devices with their start and end apart: 3 -> 3, of which waited for: 2 -> 2; matrix products, arithmetic and copies ran while one was open for 1% -> 0% of each run, Pallas kernels for 0% -> 0%
where the time goes in v1:
time: 572 us; the launch traced here: 571 us
  waiting for transfers between devices  371 us (65%)
  blocking collectives  126 us (22%)
  local copies, waits for them, and re-layouts  27.4 us (5%)
  starting transfers between devices  25.4 us (4%)
  matrix products  16.5 us (3%)
    all_to_all x1, waiting for transfers between devices, use_numbers(): lax.all_to_all(jnp.stack([tile_in for _ in range(lax.axis_size(chip_axis)...  361 us
    psum x1, blocking collectives, local(): total_squares = lax.psum(partial_squares, 'tensor')  126 us
    reshape x1, local copies, waits for them, and re-layouts, use_numbers(): jnp.concatenate(lax.all_to_all(jnp.stack([tile_in for _ in range(lax.axis...  16.8 us
    all_to_all x1, starting transfers between devices, use_numbers(): lax.all_to_all(jnp.stack([tile_in for _ in range(lax.axis_size(chip_axis)...  15.1 us
  transfers between devices with their start and end apart: 3, of which 2 were waited for; matrix products, arithmetic and copies ran while one was open for 0% of the time, Pallas kernels for 0%

profile of v1, /device:TPU:1, one launch (start us, length us, event | category | flops | bytes accessed | tf_op | source)
XLA Modules:
  0.0 571.2 jit_solution(1885289066221089834)
XLA Ops:
  0.6 0.0 copy-start
  0.6 6.8 %stack.3 = bf16[64,12,8192]{2,1,0:T(8,128)(2,1)} broadcast(bf16[12,8192]{1,0:T(8,128)(2,1)} %bitcast.32), dimensions={1,2} | broadcast | bytes 12779520 | tf_op jit(solution)/shard_map/stack | solution.py:11
  7.5 0.0 copy-start.1
  7.5 15.1 %all-to-all-start = ((bf16[64,12,8192]{2,1,0:T(8,128)(2,1)}), bf16[64,12,8192]{2,1,0:T(8,128)(2,1)}, u32[]{:S(2)}, u32[]{:S(2)}) async-start(bf16[64,12,8192]{2,1,0:T(8,128)(2,1)} %stack.3), calls=%async_computation | async-start | bytes 33554432 | tf_op jit(solution)/shard_map/all_to_all | solution.py:10
  22.6 0.0 copy-done.1
  22.6 0.1 copy.22
  22.7 0.1 eq.29
  22.9 0.1 eq.25
  23.1 0.9 reduce-window.6
  23.9 0.2 slice_reduce_fusion
  24.2 361.0 %all-to-all-done = bf16[64,12,8192]{2,1,0:T(8,128)(2,1)} async-done(((bf16[64,12,8192]{2,1,0:T(8,128)(2,1)}), bf16[64,12,8192]{2,1,0:T(8,128)(2,1)}, u32[]{:S(2)}, u32[]{:S(2)}) %all-to-all-start) | async-done | bytes 12582944 | tf_op jit(solution)/shard_map/all_to_all | solution.py:10
  385.1 16.8 %reshape.83 = bf16[768,8192]{1,0:T(8,128)(2,1)} reshape(bf16[64,12,8192]{2,1,0:T(8,128)(2,1)} %all-to-all-done) | data formatting | bytes 25165824 | tf_op jit(solution)/shard_map/reshape | solution.py:9
  402.0 0.0 copy-done
  402.0 0.0 copy-start.2
  402.0 8.6 %fusion.3 = bf16[768,96]{0,1:T(8,128)(2,1)S(1)} fusion(bf16[768,8192]{1,0:T(8,128)(2,1)} %reshape.83, bf16[1,96,8192]{2,1,0:T(8,128)(2,1)S(1)} %copy-done), kind=kOutput, calls=%fused_computation.6 | convolution fusion | flops 1208033280 | bytes 14303232 | tf_op jit(solution)/shard_map/dot_general | solution.py:37
  410.6 0.2 reshape.84
  410.8 0.7 copy.24
  411.5 6.8 %all-to-all-start.1 = ((bf16[8,96,96]{1,2,0:T(8,128)(2,1)}), bf16[8,96,96]{1,2,0:T(8,128)(2,1)S(1)}, u32[]{:S(2)}, u32[]{:S(2)}) async-start(bf16[8,96,96]{1,2,0:T(8,128)(2,1)} %copy.24), calls=%async_computation.1 | async-start | bytes 393216 | tf_op jit(solution)/shard_map/all_to_all | solution.py:41
  418.3 0.1 fusion.11
  418.4 0.1 copy.21
  418.6 0.1 mul.51
  418.7 0.0 copy-done.2
  418.7 0.1 copy.26
  418.8 0.1 mul.57
  419.0 10.2 %all-to-all-done.1 = bf16[8,96,96]{1,2,0:T(8,128)(2,1)S(1)} async-done(((bf16[8,96,96]{1,2,0:T(8,128)(2,1)}), bf16[8,96,96]{1,2,0:T(8,128)(2,1)S(1)}, u32[]{:S(2)}, u32[]{:S(2)}) %all-to-all-start.1) | async-done | bytes 147488 | tf_op jit(solution)/shard_map/all_to_all | solution.py:41
  429.2 0.1 copy.25
  429.3 1.4 gather_fusion
  430.8 0.3 fusion.6
  431.2 0.1 mul.55
  431.2 2.2 scatter_custom_fusion
  433.4 3.4 all-to-all-start.2
  436.8 0.1 multiply_reduce_fusion
  437.0 125.8 %psum.7 = f32[192]{0:T(256)S(1)} all-reduce(f32[192]{0:T(256)S(1)} %multiply_reduce_fusion), channel_id=1, replica_groups=mesh['expert'=8,'tensor'=64] {'tensor'}, use_global_device_ids=true, to_apply=%region_6.7 | all-reduce | flops 192 | bytes 1536 | tf_op jit(solution)/shard_map/psum | solution.py:66
  562.7 0.6 broadcast_multiply_fusion.1
  563.3 0.0 all-to-all-done.2
  563.3 7.9 %fusion = bf16[1,96,8192]{2,1,0:T(8,128)(2,1)} fusion(bf16[768,96]{1,0:T(8,128)(2,1)S(1)} %bitcast.29, bf16[768,8192]{1,0:T(8,128)(2,1)} %reshape.83), kind=kOutput, calls=%fused_computation.3 | convolution fusion | flops 1208745984 | bytes 14303232 | tf_op jit(solution)/shard_map/dot_general | solution.py:62
  (5 shorter events, 0.1 us)
Async XLA Ops:
  0.6 401.4 %copy-start = (bf16[1,96,8192]{2,1,0:T(8,128)(2,1)S(1)}, bf16[1,96,8192]{2,1,0:T(8,128)(2,1)}, u32[]{:S(2)}) copy-start(bf16[1,96,8192]{2,1,0:T(8,128)(2,1)} %param.5) | copy-start | bytes 4718596
  7.5 15.2 %copy-start.1 = (s32[192,2]{0,1:T(2,128)S(1)}, s32[192,2]{0,1:T(2,128)}, u32[]{:S(2)}) copy-start(s32[192,2]{0,1:T(2,128)} %param.6) | copy-start | bytes 4612
  7.5 377.7 %all-to-all-start = ((bf16[64,12,8192]{2,1,0:T(8,128)(2,1)}), bf16[64,12,8192]{2,1,0:T(8,128)(2,1)}, u32[]{:S(2)}, u32[]{:S(2)}) async-start(bf16[64,12,8192]{2,1,0:T(8,128)(2,1)} %stack.3), calls=%async_computation | async-start | bytes 33554432 | tf_op jit(solution)/shard_map/all_to_all | solution.py:10
  402.0 16.7 %copy-start.2 = (f32[192,2]{0,1:T(2,128)S(1)}, f32[192,2]{0,1:T(2,128)}, u32[]{:S(2)}) copy-start(f32[192,2]{0,1:T(2,128)} %param.7) | copy-start | bytes 4612
  411.5 17.7 %all-to-all-start.1 = ((bf16[8,96,96]{1,2,0:T(8,128)(2,1)}), bf16[8,96,96]{1,2,0:T(8,128)(2,1)S(1)}, u32[]{:S(2)}, u32[]{:S(2)}) async-start(bf16[8,96,96]{1,2,0:T(8,128)(2,1)} %copy.24), calls=%async_computation.1 | async-start | bytes 393216 | tf_op jit(solution)/shard_map/all_to_all | solution.py:41
  433.4 129.8 %all-to-all-start.2 = ((bf16[8,96,96]{2,1,0:T(8,128)(2,1)}), bf16[8,96,96]{2,1,0:T(8,128)(2,1)S(1)}, u32[]{:S(2)}, u32[]{:S(2)}) async-start(bf16[8,96,96]{2,1,0:T(8,128)(2,1)} %bitcast.7), calls=%async_computation.2 | async-start | bytes 393216 | tf_op jit(solution)/shard_map/all_to_all | solution.py:54
